TPU v7x, 256 devices: a whole 4x4x8 slice. The times are simulated.
256 devices in a mesh: ctx: 16 (over z, core), ch: 16 (over x, y).
Axes of the slice: x: 4, y: 4, z: 8, core: 2. Of those that a mesh axis runs over, the one named last changes fastest.
Arguments:
- layer_input: bfloat16 [6144, 16384], P('ctx', 'ch'), may hold values from -6 to 6
- gate_input: bfloat16 [6144, 16384], P('ctx', 'ch'), may hold values from -6 to 6
- conv_weight: float32 [4, 16384], P(None, 'ch'), may hold values from -3 to 3
- conv_bias: float32 [16384], P('ch'), may hold values from -3 to 3
- select_weight: bfloat16 [544, 16384], P(None, 'ch'), may hold values from -0.046875 to 0.046875
- step_weight: bfloat16 [512, 16384], P(None, 'ch'), may hold values from -0.25 to 0.25
- step_bias: float32 [16384], P('ch')
- decay_log: float32 [16, 16384], P(None, 'ch')
- skip_gain: float32 [16384], P('ch'), may hold values from 0.5 to 1.5
- out_weight: bfloat16 [16384, 4096], P('ch'), may hold values from -0.046875 to 0.046875
- residual: bfloat16 [6144, 4096], P('ctx', 'ch')
- norm_gain: float32 [4096], replicated, may hold values from 0.5 to 1.5
- head_weight: bfloat16 [4096, 32768], P('ctx', 'ch')
- targets: int32 [6144], P('ctx'), may hold values from 0 to 32767
Outputs:
- token_logprob: float32 [6144], P('ctx')
- mean_logprob: float32 [6144], P('ctx')
- logprob_variance: float32 [6144], P('ctx')
All inputs are finite; a program needn't handle non-finite values.
Results may differ from a plain program's by a relative error of at most 0.0051.
Values may be sent and summed in bfloat16 or wider, within the bound.
A program may use at most 128 MiB of HBM per device.

v0:
```python
import jax
import jax.numpy as jnp
from jax import lax
from jax.sharding import PartitionSpec as P

STATE = 16
RANK = 512
KCONV = 4


def from_behind(shard, axis, by):
    size = lax.axis_size(axis)
    pairs = [(i, i + by) for i in range(size) if 0 <= i + by < size]
    return lax.ppermute(shard, axis, pairs)


def sigmoid_linear(operand):
    return operand / (1.0 + jnp.exp(-operand))


def smooth_relu(operand):
    return jnp.logaddexp(operand, 0.0)


def per_device(
    layer_input,
    gate_input,
    conv_weight,
    conv_bias,
    select_weight,
    step_weight,
    step_bias,
    decay_log,
    skip_gain,
    out_weight,
    residual,
    norm_gain,
    head_weight,
    targets,
):
    tok_rows, channels = layer_input.shape
    edge_rows = from_behind(layer_input[tok_rows - (KCONV - 1) :], "ctx", 1)
    padded = jnp.concatenate([edge_rows, layer_input], axis=0).astype(jnp.float32)
    convolved = jnp.zeros((tok_rows, channels), jnp.float32) + conv_bias[None, :]
    for offset in range(KCONV):
        convolved = convolved + conv_weight[offset][None, :] * padded[offset : offset + tok_rows]
    smoothed = sigmoid_linear(convolved).astype(jnp.bfloat16)
    partial_sums = lax.dot_general(
        select_weight, smoothed, (((1,), (1,)), ((), ())), preferred_element_type=jnp.float32
    )
    projected = lax.psum(partial_sums, "ch")
    step_low = projected[:RANK].astype(jnp.bfloat16)
    state_entry = projected[RANK : RANK + STATE]
    state_readout = projected[RANK + STATE :]
    step_raw = lax.dot_general(
        step_low, step_weight, (((0,), (0,)), ((), ())), preferred_element_type=jnp.float32
    )
    step_size = smooth_relu(step_raw + step_bias[None, :])
    decay_rate = -jnp.exp(decay_log)
    smoothed_wide = smoothed.astype(jnp.float32)

    def advance(loop_carry, inputs):
        state_now, elapsed = loop_carry
        size_now, value_now, entry_now, readout_now = inputs
        state_now = (
            jnp.exp(size_now[None, :] * decay_rate) * state_now
            + (size_now * value_now)[None, :] * entry_now[:, None]
        )
        elapsed = elapsed + size_now
        return ((state_now, elapsed), (jnp.sum(readout_now[:, None] * state_now, axis=0), elapsed))

    start_carry = (jnp.zeros((STATE, channels), jnp.float32), jnp.zeros((channels,), jnp.float32))
    final_carry, outputs = lax.scan(
        advance, start_carry, (step_size, smoothed_wide, state_entry.T, state_readout.T), unroll=16
    )
    local_state, elapsed_total = final_carry
    scanned, elapsed = outputs
    through = jnp.exp(decay_rate * elapsed_total[None, :])

    def relay_step(step_index, incoming):
        return from_behind(through * incoming + local_state, "ctx", 1)

    incoming = lax.fori_loop(0, lax.axis_size("ctx") - 1, relay_step, jnp.zeros_like(local_state))
    correction = jnp.zeros_like(scanned)
    for index_state in range(STATE):
        correction = (
            correction
            + state_readout[index_state][:, None]
            * jnp.exp(decay_rate[index_state][None, :] * elapsed)
            * incoming[index_state][None, :]
        )
    mixer_input = (
        (scanned + correction + skip_gain[None, :] * smoothed_wide)
        * sigmoid_linear(gate_input.astype(jnp.float32))
    ).astype(jnp.bfloat16)
    mixer_out = lax.psum(jnp.dot(mixer_input, out_weight, preferred_element_type=jnp.float32), "ch")
    stream = lax.all_gather(residual, "ch", axis=1, tiled=True)
    hidden = stream.astype(jnp.float32) + mixer_out
    normed = (
        hidden
        * lax.rsqrt(jnp.mean(hidden * hidden, axis=1, keepdims=True) + 1e-06)
        * norm_gain[None, :]
    ).astype(jnp.bfloat16)
    vocab_cols = head_weight.shape[1]
    logits = jnp.dot(
        normed,
        lax.all_gather(head_weight, "ctx", axis=0, tiled=True),
        preferred_element_type=jnp.float32,
    )
    column = lax.broadcasted_iota(jnp.int32, logits.shape, 1) + lax.axis_index("ch") * vocab_cols
    picked = jnp.sum(jnp.where(column == targets[:, None], logits, 0.0), axis=1)
    row_peak = lax.pmax(jnp.max(logits, axis=1), "ch")
    shifted = logits - row_peak[:, None]
    weights = jnp.exp(shifted)
    row_total, row_first, row_second, picked = lax.psum(
        (
            jnp.sum(weights, axis=1),
            jnp.sum(weights * shifted, axis=1),
            jnp.sum(weights * shifted * shifted, axis=1),
            picked,
        ),
        "ch",
    )
    log_total = jnp.log(row_total)
    mean_ratio = row_first / row_total
    return (
        picked - row_peak - log_total,
        mean_ratio - log_total,
        row_second / row_total - mean_ratio * mean_ratio,
    )


def solution(mesh):
    in_specs = (
        P("ctx", "ch"),
        P("ctx", "ch"),
        P(None, "ch"),
        P("ch"),
        P(None, "ch"),
        P(None, "ch"),
        P("ch"),
        P(None, "ch"),
        P("ch"),
        P("ch", None),
        P("ctx", "ch"),
        P(),
        P("ctx", "ch"),
        P("ctx"),
    )
    out_specs = (P("ctx"), P("ctx"), P("ctx"))
    return jax.shard_map(
        per_device, mesh=mesh, in_specs=in_specs, out_specs=out_specs, check_vma=False
    )
```

profile of v0, /device:TPU:8, one launch (start us, length us, event | category | flops | bytes accessed | tf_op | source)
XLA Modules:
  0.0 688.0 jit_solution(6019642598044573003)
XLA Ops:
  8.0 1.7 collective-permute-start.1
  10.7 1.4 maximum_convert_fusion
  14.0 1.7 convolution_bitcast_fusion
  17.2 2.5 convert.6
  19.7 98.2 %all-reduce.4.cloned.1.call-done = f32[544,384]{1,0:T(8,128)} async-done(((f32[544,384]{1,0:T(8,128)}), f32[544,384]{1,0:T(8,128)}) %all-reduce.4.cloned.1.call-update) | async-done | bytes 835600 | tf_op jit(solution)/shard_map/psum | solution.py:51
  118.9 3.9 compare_select_fusion
  122.8 116.6 %while.28 = (s32[]{:T(128)}, f32[16,1024]{1,0:T(8,128)S(1)}, f32[1024]{0:T(1024)S(1)}, f32[24,16,1024]{2,1,0:T(8,128)}, f32[24,16,1024]{2,1,0:T(8,128)}, /*index...) while((s32[]{:T(128)}, f32[16,1024]{1,0:T(8,128)S(1)}, ...), condition=%wide.region_18.19_spmd.clone, body=%wide.region_1.18_spmd.clone.sunk | while | flops 2343954 | bytes 2588525 | solution.py:73
  124.1 1.3 constant_dynamic-slice_fusion.67
  128.9 1.3 constant_dynamic-slice_fusion.67
  142.1 1.5 constant_dynamic-slice_fusion.66
  143.7 1.3 constant_dynamic-slice_fusion.67
  148.5 1.3 constant_dynamic-slice_fusion.67
  152.1 1.5 constant_dynamic-slice_fusion.66
  158.4 1.3 constant_dynamic-slice_fusion.67
  172.9 1.3 constant_dynamic-slice_fusion.67
  177.7 1.3 constant_dynamic-slice_fusion.67
  187.3 1.3 constant_dynamic-slice_fusion.67
  192.2 1.3 constant_dynamic-slice_fusion.67
  197.0 1.3 constant_dynamic-slice_fusion.67
  201.9 1.5 constant_dynamic-slice_fusion.67
  211.7 1.3 constant_dynamic-slice_fusion.67
  216.6 1.3 constant_dynamic-slice_fusion.67
  226.2 1.3 constant_dynamic-slice_fusion.67
  231.1 1.3 constant_dynamic-slice_fusion.67
  240.9 80.6 %while.27 = (s32[]{:T(128)}, f32[16,1024]{1,0:T(8,128)S(1)}, f32[16,1024]{1,0:T(8,128)S(1)}, f32[16,1024]{1,0:T(8,128)S(1)}, s32[]{:T(128)}) while((s32[]{:T(128)}, f32[16,1024]{1,0:T(8,128)S(1)}, f32[16,1024]{1,0:T(8,128)S(1)}, f32[16,1024]{1,0:T(8,128)S(1)}, s32[]{:T(128)}) %tuple.214), condition=%wide.region_20.21_spmd, body=%wide.region_19.20_spmd.sunk | while | flops 32770 | bytes 524389 | solution.py:83
  243.2 4.6 collective-permute-start
  248.7 4.7 collective-permute-start
  254.3 4.7 collective-permute-start
  259.9 4.7 collective-permute-start
  265.5 4.7 collective-permute-start
  271.1 4.7 collective-permute-start
  276.7 4.7 collective-permute-start
  282.3 4.7 collective-permute-start
  287.9 4.7 collective-permute-start
  293.5 4.7 collective-permute-start
  299.1 4.7 collective-permute-start
  304.7 4.7 collective-permute-start
  310.3 4.7 collective-permute-start
  315.9 4.7 collective-permute-start
  321.7 8.7 %fusion.111 = bf16[384,1024]{1,0:T(8,128)(2,1)S(1)} fusion(bf16[384,1024]{1,0:T(8,128)(2,1)} %param.19, f32[24,16,1024]{2,1,0:T(8,128)} %get-tuple-element.81, f32[24,16,1024]{2,1,0:T(8,128)} %get-tuple-element.80, f32[1024]{0:T(1024)S(1)} %copy-done.22, f32[1024]{0:T(1024)S(1)} %bitcast.639, f32[1024]{0:T(1024)S(1)} %bitcast.637, ...), kind=kLoop, calls=%fused_computation.241 | loop fusion | flops 33423360 | bytes 11190272 | tf_op jit(solution)/shard_map/convert_element_type | solution.py:95
  330.5 5.3 fusion.117
  336.4 153.1 %all-reduce.6.cloned.1.call-done = f32[384,4096]{1,0:T(8,128)} async-done(((f32[384,4096]{1,0:T(8,128)}), f32[384,4096]{1,0:T(8,128)}) %all-reduce.6.cloned.1.call-update) | async-done | bytes 6291472 | tf_op jit(solution)/shard_map/psum | solution.py:96
  489.5 4.6 multiply_reduce_fusion.16
  494.1 92.5 %all-gather.5.cloned.1.call-done = bf16[4096,2048]{1,0:T(8,128)(2,1)} async-done(((bf16[256,2048]{1,0:T(8,128)(2,1)}), bf16[4096,2048]{1,0:T(8,128)(2,1)}) %all-gather.5.cloned.1.call-update) | async-done | bytes 16777232 | tf_op jit(solution)/shard_map/all_gather | solution.py:107
  586.6 14.3 %fusion.116 = (f32[384]{0:T(512)S(1)}, f32[384,2048]{1,0:T(8,128)}) fusion(bf16[4096,2048]{1,0:T(8,128)(2,1)} %all-gather.5.cloned.1.call-done, f32[384,4096]{1,0:T(8,128)} %all-reduce.6.cloned.1.call-done, bf16[384,4096]{1,0:T(8,128)(2,1)} %all-gather.3.cloned.1.call-done, f32[4096]{0:T(1024)S(1)} %copy-done.20, f32[384]{0:T(512)S(1)} %add_rsqrt_fusion), kind=kOutput, calls=%fused_computation.274 | convolution fusion | flops 6451101184 | bytes 29379584 | tf_op jit(solution)/shard_map/dot_general | solution.py:105
  600.9 36.3 %pmax.7 = f32[384]{0:T(512)S(1)} all-reduce(f32[384]{0:T(512)S(1)} %get-tuple-element.335), channel_id=1, replica_groups=mesh['ctx'=16,'ch'=16] {'ch'}, use_global_device_ids=true, to_apply=%region_26.27 | all-reduce | flops 384 | bytes 3072 | tf_op jit(solution)/shard_map/pmax | solution.py:112
  637.2 3.2 fusion.35
  640.5 40.4 %all-reduce = (f32[384]{0:T(512)S(1)}, f32[384]{0:T(512)S(1)}, f32[384]{0:T(512)S(1)}, f32[384]{0:T(512)S(1)}) all-reduce(f32[384]{0:T(512)S(1)} %get-tuple-element.156, f32[384]{0:T(512)S(1)} %get-tuple-element.155, f32[384]{0:T(512)S(1)} %get-tuple-element.154, ...), channel_id=1, replica_groups=mesh['ctx'=16,'ch'=16] {'ch'}, use_global_device_ids=true, to_apply=%region_24.25 | all-reduce | flops 1536 | bytes 12288 | tf_op jit(solution)/shard_map/psum | solution.py:115
  (785 shorter events, 112.9 us)
Async XLA Ops:
  7.2 6.8 copy-start
  7.2 4.9 copy-start.3
  7.2 110.7 %all-reduce.4.cloned.1.call-start = ((), (), s32[]{:S(2)}) async-start(), calls=%async_computation.1 | async-start | bytes 1671168 | tf_op jit(solution)/shard_map/psum | solution.py:51
  8.0 2.6 collective-permute-start.1
  13.1 0.9 copy-start.1
  14.0 2.5 copy-start.2
  15.7 320.7 %all-gather.3.cloned.1.call-start = ((), (), s32[]{:S(2)}) async-start(), calls=%async_computation | async-start | bytes 3342336 | tf_op jit(solution)/shard_map/all_gather | solution.py:97
  16.4 473.1 %all-reduce.6.cloned.1.call-start = ((), (), s32[]{:S(2)}) async-start(), calls=%async_computation.2 | async-start | bytes 12582912 | tf_op jit(solution)/shard_map/psum | solution.py:96
  16.5 102.4 %copy-start.21 = (f32[1024]{0:T(1024)S(1)}, f32[1024]{0:T(1024)}, u32[]{:S(2)}) copy-start(f32[1024]{0:T(1024)} %param.24) | copy-start | bytes 12292
  239.5 82.1 %copy-start.4 = (f32[1,1024]{1,0:T(1,128)S(1)}, f32[1,1024]{1,0:T(1,128)}, u32[]{:S(2)}) copy-start(f32[1,1024]{1,0:T(1,128)} %get-tuple-element.298) | copy-start | bytes 12292
  239.5 82.1 %copy-start.5 = (f32[1,1024]{1,0:T(1,128)S(1)}, f32[1,1024]{1,0:T(1,128)}, u32[]{:S(2)}) copy-start(f32[1,1024]{1,0:T(1,128)} %get-tuple-element.299) | copy-start | bytes 12292
  239.5 82.1 %copy-start.6 = (f32[1,1024]{1,0:T(1,128)S(1)}, f32[1,1024]{1,0:T(1,128)}, u32[]{:S(2)}) copy-start(f32[1,1024]{1,0:T(1,128)} %get-tuple-element.300) | copy-start | bytes 12292
  239.5 82.1 %copy-start.7 = (f32[1,1024]{1,0:T(1,128)S(1)}, f32[1,1024]{1,0:T(1,128)}, u32[]{:S(2)}) copy-start(f32[1,1024]{1,0:T(1,128)} %get-tuple-element.301) | copy-start | bytes 12292
  239.5 82.1 %copy-start.8 = (f32[1,1024]{1,0:T(1,128)S(1)}, f32[1,1024]{1,0:T(1,128)}, u32[]{:S(2)}) copy-start(f32[1,1024]{1,0:T(1,128)} %get-tuple-element.302) | copy-start | bytes 12292
  239.5 82.1 %copy-start.9 = (f32[1,1024]{1,0:T(1,128)S(1)}, f32[1,1024]{1,0:T(1,128)}, u32[]{:S(2)}) copy-start(f32[1,1024]{1,0:T(1,128)} %get-tuple-element.303) | copy-start | bytes 12292
  239.5 82.1 %copy-start.10 = (f32[1,1024]{1,0:T(1,128)S(1)}, f32[1,1024]{1,0:T(1,128)}, u32[]{:S(2)}) copy-start(f32[1,1024]{1,0:T(1,128)} %get-tuple-element.304) | copy-start | bytes 12292
  239.5 82.1 %copy-start.11 = (f32[1,1024]{1,0:T(1,128)S(1)}, f32[1,1024]{1,0:T(1,128)}, u32[]{:S(2)}) copy-start(f32[1,1024]{1,0:T(1,128)} %get-tuple-element.305) | copy-start | bytes 12292
  239.5 82.1 %copy-start.12 = (f32[1,1024]{1,0:T(1,128)S(1)}, f32[1,1024]{1,0:T(1,128)}, u32[]{:S(2)}) copy-start(f32[1,1024]{1,0:T(1,128)} %get-tuple-element.306) | copy-start | bytes 12292
  239.5 82.1 %copy-start.13 = (f32[1,1024]{1,0:T(1,128)S(1)}, f32[1,1024]{1,0:T(1,128)}, u32[]{:S(2)}) copy-start(f32[1,1024]{1,0:T(1,128)} %get-tuple-element.307) | copy-start | bytes 12292
  239.5 82.1 %copy-start.14 = (f32[1,1024]{1,0:T(1,128)S(1)}, f32[1,1024]{1,0:T(1,128)}, u32[]{:S(2)}) copy-start(f32[1,1024]{1,0:T(1,128)} %get-tuple-element.308) | copy-start | bytes 12292
  239.6 82.1 %copy-start.15 = (f32[1,1024]{1,0:T(1,128)S(1)}, f32[1,1024]{1,0:T(1,128)}, u32[]{:S(2)}) copy-start(f32[1,1024]{1,0:T(1,128)} %get-tuple-element.309) | copy-start | bytes 12292
  239.6 82.1 %copy-start.16 = (f32[1,1024]{1,0:T(1,128)S(1)}, f32[1,1024]{1,0:T(1,128)}, u32[]{:S(2)}) copy-start(f32[1,1024]{1,0:T(1,128)} %get-tuple-element.310) | copy-start | bytes 12292
  239.6 82.1 %copy-start.17 = (f32[1,1024]{1,0:T(1,128)S(1)}, f32[1,1024]{1,0:T(1,128)}, u32[]{:S(2)}) copy-start(f32[1,1024]{1,0:T(1,128)} %get-tuple-element.311) | copy-start | bytes 12292
  239.6 82.1 %copy-start.22 = (f32[1024]{0:T(1024)S(1)}, f32[1024]{0:T(1024)}, u32[]{:S(2)}) copy-start(f32[1024]{0:T(1024)} %param.26) | copy-start | bytes 12292
  241.0 2.2 collective-permute-start
  243.2 5.5 collective-permute-start
  248.7 5.6 collective-permute-start
  254.3 5.6 collective-permute-start
  259.9 5.6 collective-permute-start
  265.5 5.6 collective-permute-start
  271.1 5.6 collective-permute-start
  276.7 5.6 collective-permute-start
  282.3 5.6 collective-permute-start
  287.9 5.6 collective-permute-start
  293.5 5.6 collective-permute-start
  299.1 5.6 collective-permute-start
  304.7 5.6 collective-permute-start
  310.3 5.6 collective-permute-start
  315.9 5.6 collective-permute-start
  321.7 8.7 %copy-start.19 = (bf16[1024,4096]{1,0:T(8,128)(2,1)S(1)}, bf16[1024,4096]{1,0:T(8,128)(2,1)}, u32[]{:S(2)}) copy-start(bf16[1024,4096]{1,0:T(8,128)(2,1)} %param.27) | copy-start | bytes 25165828
  335.7 250.9 %all-gather.5.cloned.1.call-start = ((), (), s32[]{:S(2)}) async-start(), calls=%async_computation.3 | async-start | bytes 17825792 | tf_op jit(solution)/shard_map/all_gather | solution.py:107
  336.3 250.3 %copy-start.20 = (f32[4096]{0:T(1024)S(1)}, f32[4096]{0:T(1024)}, u32[]{:S(2)}) copy-start(f32[4096]{0:T(1024)} %param.29) | copy-start | bytes 49156
  494.1 143.1 %copy-start.18 = (s32[384]{0:T(512)S(1)}, s32[384]{0:T(512)}, u32[]{:S(2)}) copy-start(s32[384]{0:T(512)} %param.31) | copy-start | bytes 4612
Sparse Core Ops, SparseCore 0:
  15.8 102.0 all-reduce.3
  120.3 56.3 all-gather.2
  335.9 153.5 all-reduce.5
  491.2 95.4 all-gather.4
where the time goes:
time: 694 us; the launch traced here: 688 us
  waiting for transfers between devices  358 us (52%)
  local copies, waits for them, and re-layouts  95.7 us (14%)
  blocking collectives  76.8 us (11%)
  starting transfers between devices  69 us (10%)
  other arithmetic  45 us (6%)
  matrix products  25.1 us (4%)
  between operations  14.2 us (2%)
    psum x1, waiting for transfers between devices, per_device(): lax.psum(jnp.dot(mixer_input, out_weight, preferred_element_type=jnp.floa...  153 us
    psum x1, waiting for transfers between devices, per_device(): projected = lax.psum(partial_sums, 'ch')  98.2 us
    all_gather x1, waiting for transfers between devices, per_device(): lax.all_gather(head_weight, 'ctx', axis=0, tiled=True)  92.5 us
    ppermute x16, starting transfers between devices, from_behind(): return lax.ppermute(shard, axis, pairs)  68.7 us
    slice x48, local copies, waits for them, and re-layouts, per_device(): lax.scan(advance, start_carry, (step_size, smoothed_wide, state_entry.T,...  63.6 us
    psum x1, blocking collectives, per_device(): lax.psum((jnp.sum(weights, axis=1), jnp.sum(weights * shifted, axis=1), j...  40.4 us
    pmax x1, blocking collectives, per_device(): row_peak = lax.pmax(jnp.max(logits, axis=1), 'ch')  36.3 us
    reduce_sum x120, other arithmetic, advance(): jnp.sum(readout_now[:, None] * state_now, axis=0)  19.8 us
  transfers between devices with their start and end apart: 20, of which 18 were waited for; matrix products, arithmetic and copies ran while one was open for 21% of the time, Pallas kernels for 0%

commit v1 on v0

--- a/solution.py
+++ b/solution.py
@@ -104,7 +104,9 @@
     vocab_cols = head_weight.shape[1]
     logits = jnp.dot(
         normed,
-        lax.all_gather(head_weight, "ctx", axis=0, tiled=True),
+        jnp.concatenate(
+            lax.all_to_all(jnp.stack([head_weight] * lax.axis_size("ctx")), "ctx", 0, 0), axis=0
+        ),
         preferred_element_type=jnp.float32,
     )
     column = lax.broadcasted_iota(jnp.int32, logits.shape, 1) + lax.axis_index("ch") * vocab_cols

time: 694 us -> 753 us (1.085)
  starting transfers between devices: 69 us -> 232 us
  waiting for transfers between devices: 358 us -> 247 us
    ppermute x16, starting transfers between devices: 68.7 us -> 220 us  [from_behind(): return lax.ppermute(shard, axis, pairs)]
    all_gather x1 -> x0, waiting for transfers between devices: 92.5 us -> none  [per_device(): lax.all_gather(head_weight, 'ctx', axis=0, tiled=True)]
    psum x1, waiting for transfers between devices: 98.2 us -> 80 us  [per_device(): projected = lax.psum(partial_sums, 'ch')]
    all_to_all x0 -> x1, starting transfers between devices: none -> 12.3 us  [per_device(): lax.all_to_all(jnp.stack([head_weight] * lax.axis_size('ctx')), 'ctx', 0, 0)]
  transfers between devices with their start and end apart: 20 -> 20, of which waited for: 18 -> 17; matrix products, arithmetic and copies ran while one was open for 21% -> 20% of each run, Pallas kernels for 0% -> 0%
where the time goes in v1:
time: 753 us; the launch traced here: 747 us
  waiting for transfers between devices  247 us (33%)
  starting transfers between devices  232 us (31%)
  local copies, waits for them, and re-layouts  102 us (14%)
  blocking collectives  75.1 us (10%)
  other arithmetic  43.7 us (6%)
  matrix products  28.5 us (4%)
  between operations  14.1 us (2%)
    ppermute x16, starting transfers between devices, from_behind(): return lax.ppermute(shard, axis, pairs)  220 us
    psum x1, waiting for transfers between devices, per_device(): lax.psum(jnp.dot(mixer_input, out_weight, preferred_element_type=jnp.floa...  154 us
    psum x1, waiting for transfers between devices, per_device(): projected = lax.psum(partial_sums, 'ch')  80 us
    slice x48, local copies, waits for them, and re-layouts, per_device(): lax.scan(advance, start_carry, (step_size, smoothed_wide, state_entry.T,...  65 us
    psum x1, blocking collectives, per_device(): lax.psum((jnp.sum(weights, axis=1), jnp.sum(weights * shifted, axis=1), j...  38.9 us
    pmax x1, blocking collectives, per_device(): row_peak = lax.pmax(jnp.max(logits, axis=1), 'ch')  36.2 us
    reduce_sum x120, other arithmetic, advance(): jnp.sum(readout_now[:, None] * state_now, axis=0)  19.7 us
    dynamic_update_slice x24, local copies, waits for them, and re-layouts, per_device(): lax.scan(advance, start_carry, (step_size, smoothed_wide, state_entry.T,...  15.8 us
  transfers between devices with their start and end apart: 20, of which 17 were waited for; matrix products, arithmetic and copies ran while one was open for 20% of the time, Pallas kernels for 0%

profile of v1, /device:TPU:8, one launch (start us, length us, event | category | flops | bytes accessed | tf_op | source)
XLA Modules:
  0.0 747.0 jit_solution(2910671968938132205)
XLA Ops:
  8.0 1.7 collective-permute-start.1
  10.7 1.4 maximum_convert_fusion
  13.1 1.7 convolution_bitcast_fusion
  14.8 6.9 stack.2
  21.7 12.3 %all-to-all-start = ((bf16[16,256,2048]{2,1,0:T(8,128)(2,1)}), bf16[16,256,2048]{2,1,0:T(8,128)(2,1)}, u32[]{:S(2)}, u32[]{:S(2)}) async-start(bf16[16,256,2048]{2,1,0:T(8,128)(2,1)} %stack.2), calls=%async_computation | async-start | bytes 33554432 | tf_op jit(solution)/shard_map/all_to_all | solution.py:108
  37.0 80.0 %all-reduce.4.cloned.1.call-done = f32[544,384]{1,0:T(8,128)} async-done(((f32[544,384]{1,0:T(8,128)}), f32[544,384]{1,0:T(8,128)}) %all-reduce.4.cloned.1.call-update) | async-done | bytes 835600 | tf_op jit(solution)/shard_map/psum | solution.py:51
  118.0 3.9 compare_select_fusion
  121.9 116.7 %while.28 = (s32[]{:T(128)}, f32[16,1024]{1,0:T(8,128)S(1)}, f32[1024]{0:T(1024)S(1)}, f32[24,16,1024]{2,1,0:T(8,128)}, f32[24,16,1024]{2,1,0:T(8,128)}, /*index...) while((s32[]{:T(128)}, f32[16,1024]{1,0:T(8,128)S(1)}, ...), condition=%wide.region_18.19_spmd.clone, body=%wide.region_1.18_spmd.clone.sunk | while | flops 2343954 | bytes 2588025 | solution.py:73
  126.8 1.3 constant_dynamic-slice_fusion.66
  128.2 1.3 constant_dynamic-slice_fusion.67
  141.3 1.3 constant_dynamic-slice_fusion.66
  146.2 1.3 constant_dynamic-slice_fusion.66
  147.5 1.4 constant_dynamic-slice_fusion.67
  155.9 1.3 constant_dynamic-slice_fusion.66
  165.5 1.3 constant_dynamic-slice_fusion.66
  175.1 1.3 constant_dynamic-slice_fusion.66
  186.1 1.5 constant_dynamic-slice_fusion.67
  189.8 1.3 constant_dynamic-slice_fusion.66
  191.2 1.3 constant_dynamic-slice_fusion.67
  194.7 1.6 constant_dynamic-slice_fusion.66
  205.9 1.4 constant_dynamic-slice_fusion.67
  210.8 1.6 constant_dynamic-slice_fusion.67
  220.7 1.3 constant_dynamic-slice_fusion.67
  225.5 1.3 constant_dynamic-slice_fusion.67
  229.0 1.3 constant_dynamic-slice_fusion.66
  239.9 231.5 %while.27 = (s32[]{:T(128)}, f32[16,1024]{1,0:T(8,128)S(1)}, f32[16,1024]{1,0:T(8,128)S(1)}, f32[16,1024]{1,0:T(8,128)S(1)}, s32[]{:T(128)}) while((s32[]{:T(128)}, f32[16,1024]{1,0:T(8,128)S(1)}, f32[16,1024]{1,0:T(8,128)S(1)}, f32[16,1024]{1,0:T(8,128)S(1)}, s32[]{:T(128)}) %tuple.214), condition=%wide.region_20.21_spmd, body=%wide.region_19.20_spmd.sunk | while | flops 32770 | bytes 524389 | solution.py:83
  242.1 155.5 %collective-permute-start = (f32[16,1024]{1,0:T(8,128)S(1)}, f32[16,1024]{1,0:T(8,128)S(1)}, u32[]{:S(2)}, u32[]{:S(2)}) collective-permute-start(f32[16,1024]{1,0:T(8,128)S(1)} %multiply_add_fusion.22), channel_id=1, source_target_pairs={{0,16},{16,32},{32,48},{48,64},{64,80},{80,96},{96,112},{112,128},... | collective-permute-start | bytes 196616 | tf_op jit(solution)/shard_map/while/body/eval_jaxpr/ppermute | solution.py:14
  398.5 4.8 collective-permute-start
  404.2 4.7 collective-permute-start
  409.9 4.7 collective-permute-start
  415.5 4.7 collective-permute-start
  421.1 4.7 collective-permute-start
  426.7 4.7 collective-permute-start
  432.3 4.7 collective-permute-start
  437.9 4.7 collective-permute-start
  443.5 4.7 collective-permute-start
  449.1 4.7 collective-permute-start
  454.7 4.7 collective-permute-start
  460.3 4.7 collective-permute-start
  465.9 4.7 collective-permute-start
  471.6 8.6 %fusion.111 = bf16[384,1024]{1,0:T(8,128)(2,1)S(1)} fusion(bf16[384,1024]{1,0:T(8,128)(2,1)} %param.19, f32[24,16,1024]{2,1,0:T(8,128)} %get-tuple-element.81, f32[24,16,1024]{2,1,0:T(8,128)} %get-tuple-element.80, f32[1024]{0:T(1024)S(1)} %copy-done.17, f32[1024]{0:T(1024)S(1)} %bitcast.640, f32[1024]{0:T(1024)S(1)} %bitcast.638, ...), kind=kLoop, calls=%fused_computation.241 | loop fusion | flops 33423360 | bytes 11190272 | tf_op jit(solution)/shard_map/convert_element_type | solution.py:95
  480.2 8.6 %fusion.117 = f32[384,4096]{1,0:T(8,128)} fusion(bf16[384,1024]{1,0:T(8,128)(2,1)S(1)} %fusion.111, bf16[1024,4096]{1,0:T(8,128)(2,1)} %param.27), kind=kOutput, calls=%fused_computation.275 | convolution fusion | flops 3221225472 | bytes 15466496 | tf_op jit(solution)/shard_map/dot_general | solution.py:96
  488.9 153.6 %all-reduce.6.cloned.1.call-done = f32[384,4096]{1,0:T(8,128)} async-done(((f32[384,4096]{1,0:T(8,128)}), f32[384,4096]{1,0:T(8,128)}) %all-reduce.6.cloned.1.call-update) | async-done | bytes 6291472 | tf_op jit(solution)/shard_map/psum | solution.py:96
  642.5 4.6 multiply_reduce_fusion.16
  647.1 14.3 %fusion.116 = (f32[384]{0:T(512)S(1)}, f32[384,2048]{1,0:T(8,128)}) fusion(bf16[4096,2048]{1,0:T(8,128)(2,1)} %bitcast.45, f32[384,4096]{1,0:T(8,128)} %all-reduce.6.cloned.1.call-done, bf16[384,4096]{1,0:T(8,128)(2,1)} %all-gather.2.cloned.1.call-done, f32[4096]{0:T(1024)S(1)} %copy-done.15, f32[384]{0:T(512)S(1)} %add_rsqrt_fusion), kind=kOutput, calls=%fused_computation.274 | convolution fusion | flops 6451101184 | bytes 29379584 | tf_op jit(solution)/shard_map/dot_general | solution.py:105
  661.4 36.2 %pmax.7 = f32[384]{0:T(512)S(1)} all-reduce(f32[384]{0:T(512)S(1)} %get-tuple-element.335), channel_id=1, replica_groups=mesh['ctx'=16,'ch'=16] {'ch'}, use_global_device_ids=true, to_apply=%region_26.27 | all-reduce | flops 384 | bytes 3072 | tf_op jit(solution)/shard_map/pmax | solution.py:114
  697.6 3.3 fusion.35
  700.9 38.9 %all-reduce = (f32[384]{0:T(512)S(1)}, f32[384]{0:T(512)S(1)}, f32[384]{0:T(512)S(1)}, f32[384]{0:T(512)S(1)}) all-reduce(f32[384]{0:T(512)S(1)} %get-tuple-element.156, f32[384]{0:T(512)S(1)} %get-tuple-element.155, f32[384]{0:T(512)S(1)} %get-tuple-element.154, ...), channel_id=1, replica_groups=mesh['ctx'=16,'ch'=16] {'ch'}, use_global_device_ids=true, to_apply=%region_24.25 | all-reduce | flops 1536 | bytes 12288 | tf_op jit(solution)/shard_map/psum | solution.py:117
  (775 shorter events, 112.5 us)
Async XLA Ops:
  7.2 5.9 copy-start
  7.2 4.9 copy-start.4
  7.2 109.8 %all-reduce.4.cloned.1.call-start = ((), (), s32[]{:S(2)}) async-start(), calls=%async_computation.2 | async-start | bytes 1671168 | tf_op jit(solution)/shard_map/psum | solution.py:51
  8.0 2.6 collective-permute-start.1
  21.7 13.3 %copy-start.2 = (f32[16,1024]{1,0:T(8,128)S(1)}, f32[16,1024]{1,0:T(8,128)}, u32[]{:S(2)}) copy-start(f32[16,1024]{1,0:T(8,128)} %param.25) | copy-start | bytes 196612
  21.7 625.4 %all-to-all-start = ((bf16[16,256,2048]{2,1,0:T(8,128)(2,1)}), bf16[16,256,2048]{2,1,0:T(8,128)(2,1)}, u32[]{:S(2)}, u32[]{:S(2)}) async-start(bf16[16,256,2048]{2,1,0:T(8,128)(2,1)} %stack.2), calls=%async_computation | async-start | bytes 33554432 | tf_op jit(solution)/shard_map/all_to_all | solution.py:108
  34.0 454.9 %all-gather.2.cloned.1.call-start = ((), (), s32[]{:S(2)}) async-start(), calls=%async_computation.1 | async-start | bytes 3342336 | tf_op jit(solution)/shard_map/all_gather | solution.py:97
  34.7 607.7 %all-reduce.6.cloned.1.call-start = ((), (), s32[]{:S(2)}) async-start(), calls=%async_computation.3 | async-start | bytes 12582912 | tf_op jit(solution)/shard_map/psum | solution.py:96
  35.0 83.0 %copy-start.16 = (f32[1024]{0:T(1024)S(1)}, f32[1024]{0:T(1024)}, u32[]{:S(2)}) copy-start(f32[1024]{0:T(1024)} %param.24) | copy-start | bytes 12292
  121.9 118.0 %copy-start.3 = (f32[16,1024]{1,0:T(8,128)S(1)}, f32[16,1024]{1,0:T(8,128)}, u32[]{:S(2)}) copy-start(f32[16,1024]{1,0:T(8,128)} %param.25) | copy-start | bytes 196612
  238.6 233.0 %copy-start.5 = (f32[1,1024]{1,0:T(1,128)S(1)}, f32[1,1024]{1,0:T(1,128)}, u32[]{:S(2)}) copy-start(f32[1,1024]{1,0:T(1,128)} %get-tuple-element.303) | copy-start | bytes 12292
  238.6 233.0 %copy-start.6 = (f32[1,1024]{1,0:T(1,128)S(1)}, f32[1,1024]{1,0:T(1,128)}, u32[]{:S(2)}) copy-start(f32[1,1024]{1,0:T(1,128)} %get-tuple-element.304) | copy-start | bytes 12292
  238.6 233.0 %copy-start.7 = (f32[1,1024]{1,0:T(1,128)S(1)}, f32[1,1024]{1,0:T(1,128)}, u32[]{:S(2)}) copy-start(f32[1,1024]{1,0:T(1,128)} %get-tuple-element.305) | copy-start | bytes 12292
  238.6 233.0 %copy-start.8 = (f32[1,1024]{1,0:T(1,128)S(1)}, f32[1,1024]{1,0:T(1,128)}, u32[]{:S(2)}) copy-start(f32[1,1024]{1,0:T(1,128)} %get-tuple-element.306) | copy-start | bytes 12292
  238.6 233.0 %copy-start.9 = (f32[1,1024]{1,0:T(1,128)S(1)}, f32[1,1024]{1,0:T(1,128)}, u32[]{:S(2)}) copy-start(f32[1,1024]{1,0:T(1,128)} %get-tuple-element.307) | copy-start | bytes 12292
  238.6 233.0 %copy-start.10 = (f32[1,1024]{1,0:T(1,128)S(1)}, f32[1,1024]{1,0:T(1,128)}, u32[]{:S(2)}) copy-start(f32[1,1024]{1,0:T(1,128)} %get-tuple-element.308) | copy-start | bytes 12292
  238.6 233.0 %copy-start.11 = (f32[1,1024]{1,0:T(1,128)S(1)}, f32[1,1024]{1,0:T(1,128)}, u32[]{:S(2)}) copy-start(f32[1,1024]{1,0:T(1,128)} %get-tuple-element.309) | copy-start | bytes 12292
  238.6 233.0 %copy-start.12 = (f32[1,1024]{1,0:T(1,128)S(1)}, f32[1,1024]{1,0:T(1,128)}, u32[]{:S(2)}) copy-start(f32[1,1024]{1,0:T(1,128)} %get-tuple-element.310) | copy-start | bytes 12292
  238.6 233.0 %copy-start.13 = (f32[1,1024]{1,0:T(1,128)S(1)}, f32[1,1024]{1,0:T(1,128)}, u32[]{:S(2)}) copy-start(f32[1,1024]{1,0:T(1,128)} %get-tuple-element.311) | copy-start | bytes 12292
  238.6 233.0 %copy-start.17 = (f32[1024]{0:T(1024)S(1)}, f32[1024]{0:T(1024)}, u32[]{:S(2)}) copy-start(f32[1024]{0:T(1024)} %param.26) | copy-start | bytes 12292
  239.9 2.2 collective-permute-start
  242.1 156.4 %collective-permute-start = (f32[16,1024]{1,0:T(8,128)S(1)}, f32[16,1024]{1,0:T(8,128)S(1)}, u32[]{:S(2)}, u32[]{:S(2)}) collective-permute-start(f32[16,1024]{1,0:T(8,128)S(1)} %multiply_add_fusion.22), channel_id=1, source_target_pairs={{0,16},{16,32},{32,48},{48,64},{64,80},{80,96},{96,112},{112,128},... | collective-permute-start | bytes 196616 | tf_op jit(solution)/shard_map/while/body/eval_jaxpr/ppermute | solution.py:14
  398.5 5.7 collective-permute-start
  404.2 5.6 collective-permute-start
  409.9 5.6 collective-permute-start
  415.5 5.6 collective-permute-start
  421.1 5.6 collective-permute-start
  426.7 5.6 collective-permute-start
  432.3 5.6 collective-permute-start
  437.9 5.6 collective-permute-start
  443.5 5.6 collective-permute-start
  449.1 5.6 collective-permute-start
  454.7 5.6 collective-permute-start
  460.3 5.6 collective-permute-start
  465.9 5.6 collective-permute-start
  488.8 158.3 %copy-start.15 = (f32[4096]{0:T(1024)S(1)}, f32[4096]{0:T(1024)}, u32[]{:S(2)}) copy-start(f32[4096]{0:T(1024)} %param.29) | copy-start | bytes 49156
  647.1 50.5 %copy-start.14 = (s32[384]{0:T(512)S(1)}, s32[384]{0:T(512)}, u32[]{:S(2)}) copy-start(s32[384]{0:T(512)} %param.31) | copy-start | bytes 4612
  697.6 42.8 %copy-start.1 = (bf16[544,1024]{1,0:T(8,128)(2,1)S(1)}, bf16[544,1024]{1,0:T(8,128)(2,1)}, u32[]{:S(2)}) copy-start(bf16[544,1024]{1,0:T(8,128)(2,1)} %param.22) | copy-start | bytes 3342340
Sparse Core Ops, SparseCore 0:
  14.9 101.9 all-reduce.3
  119.4 56.4 all-gather.1
  488.9 153.4 all-reduce.5
